TPU v7x, 32 devices: a whole 2x2x4 slice. The times are simulated.
32 devices in a mesh: batch: 8 (over z, core), critic: 4 (over y, x).
Axes of the slice: x: 2, y: 2, z: 4, core: 2. Of those that a mesh axis runs over, the one named last changes fastest.
Arguments:
- latents: bfloat16 [64, 16, 4096], P('batch', None, 'critic'), may hold values from -128 to 128
- dest: int32 [64], P('batch'), may hold values from 0 to 63, each once
- ends: int32 [64], P('batch'), may hold values from 1 to 16
- rewards: float32 [64, 16], P('batch'), may hold values from -6 to 6
- actions: int32 [64, 16], P('batch'), may hold values from 0 to 255
- w_in: bfloat16 [4, 4096, 8192], P('critic', None, 'batch'), may hold values from -1 to 1
- b_in: float32 [4, 8192], P('critic', 'batch'), may hold values from -2 to 2
- w_out: bfloat16 [4, 8192, 255], P('critic', 'batch'), may hold values from -2 to 2
- actor_w: bfloat16 [4096, 256], replicated, may hold values from -0.1875 to 0.1875
Outputs:
- critic_values: float32 [4, 64, 16], P('critic', 'batch')
- advantages: float32 [64, 16], P('batch')
- actor_grad: float32 [4096, 256], P(('batch', 'critic'))
Inputs may be any that keep to these rules, and one draw needn't show every extreme that they name: `dest`: a permutation of all learner rows.
All inputs are finite; a program needn't handle non-finite values.
Results may differ from a plain program's by a relative error of at most 0.0049.
The roundings to bfloat16 on the way count: a program that leaves them out, or rounds other values in their place, can miss the bound.
Values may be sent and summed in bfloat16 or wider, within the bound.
A program may use at most 128 MiB of HBM per device.

v0:
```python
import functools

import jax
import jax.numpy as jnp
from jax import lax
from jax.experimental import pallas as pl
from jax.experimental.pallas import tpu as pltpu
from jax.sharding import PartitionSpec as P

smoothing_heat_factor = 0.2
future_decay_factor = 0.985
blend = 0.95
MESH = pl.DeviceIdType.MESH
f32 = jnp.float32
bf16 = jnp.bfloat16
HIGHEST = lax.Precision.HIGHEST


def iota(shape, axis):
    return lax.broadcasted_iota(jnp.int32, shape, axis)


def kernel(
    sizes, lat, dest, ends, rewards, actions, w_hbm, b_in, w_out, aw_hbm,
    cv_out, adv_out, grad_out,
    xbuf, wv, awv, wov, acc, pm, lg, psum, rsib, rz, meta, metabuf, metag,
    vown, vbuf, pay, sbuf, gtmp,
    wsem, lsem, zs, zr, xs, xr, ss, sr, ps, pr, qs, qr, ms, mr, vs, vr, bs, br,
):
    nb, n, ny, nx, horizon, bins_n = sizes
    nz = nb // 2
    rows, cols = lat.shape
    half = rows // 2
    traj = rows // horizon
    total = nb * traj
    b = lax.axis_index("batch")
    c = lax.axis_index("critic")
    z, k = b // 2, b % 2
    y, x = c // nx, c % nx
    sib = z * 2 + (1 - k)
    sends = []

    def batch_peer(d):
        return ((b + d) % nb, c)

    def crit(by, bx):
        return ((y + by) % ny) * nx + (x + bx) % nx

    def weight_copy(rc):
        cc = crit(*rc)
        return (
            pltpu.make_async_copy(
                w_hbm.at[pl.ds(pl.multiple_of(cc * cols, cols), cols)],
                wv.at[pl.ds(pl.multiple_of(cc * cols, cols), cols)],
                wsem.at[rc[0] * nx + rc[1]],
            )
        )

    rel = [(by, bx) for by in range(ny) for bx in range(nx)]
    for rc in rel:
        weight_copy(rc).start()
    aw_copy = pltpu.make_async_copy(aw_hbm, awv, lsem.at[0])
    aw_copy.start()
    own_copy = pltpu.make_async_copy(lat, xbuf.at[z, c, k], lsem.at[1])
    own_copy.start()

    barrier = pltpu.get_barrier_semaphore()
    for d in range(1, nb):
        pl.semaphore_signal(barrier, inc=1, device_id=batch_peer(d), device_id_type=MESH)
    for rc in rel[1:]:
        pl.semaphore_signal(barrier, inc=1, device_id=(b, crit(*rc)), device_id_type=MESH)
    pl.semaphore_wait(barrier, nb - 1 + n - 1)

    def send(src, dst, s, r, dev):
        d = pltpu.make_async_remote_copy(
            src_ref=src, dst_ref=dst, send_sem=s, recv_sem=r, device_id=dev, device_id_type=MESH
        )
        d.start()
        sends.append(d)

    def recv(dst, s, r):
        pltpu.make_async_remote_copy(
            src_ref=dst, dst_ref=dst, send_sem=s, recv_sem=r,
            device_id=(sib, c), device_id_type=MESH,
        ).wait_recv()

    count = [0]

    def zc(dz):
        return (z + dz) % nz

    def hrow(h):
        return pl.ds(h * half, half)

    def xsem(dz, rc, h):
        return (dz * n + rc[0] * nx + rc[1]) * 2 + h

    def ssem(dz, rc):
        return dz * n + rc[0] * nx + rc[1]

    def xsend(dz, rc, h, t):
        at = xbuf.at[zc(dz), crit(*rc), k, hrow(h)]
        src = lat.at[hrow(h)] if dz == 0 and rc == (0, 0) else at
        there = ((rc[0] - t[0]) % ny, (rc[1] - t[1]) % nx)
        send(src, at, xs.at[count[0]], xr.at[xsem(dz, there, h)], (b, crit(*t)))
        count[0] += 1

    def xrecv(dz, rc, h):
        i = xsem(dz, rc, h)
        recv(xbuf.at[zc(dz), crit(*rc), k, hrow(h)], xs.at[0], xr.at[i])

    def relay(dz, rc):
        at = xbuf.at[zc(dz), crit(*rc), k]
        src = lat if dz == 0 and rc == (0, 0) else at
        send(src, at, ss.at[ssem(dz, rc)], sr.at[ssem(dz, rc)], (sib, c))

    def enter(dz):
        if dz > 0:
            recv(xbuf.at[zc(dz), c, k], zs.at[dz], zr.at[dz])
        for o in range(2):
            for tx in range(1, nx):
                xsend(dz, (0, 0), o, (0, tx))
            for ty in range(1, ny):
                xsend(dz, (0, 0), 1 - o, (ty, 0))
        relay(dz, (0, 0))

    def middle(dz):
        for bx in range(1, nx):
            xrecv(dz, (0, bx), 0)
            for ty in range(1, ny):
                xsend(dz, (0, bx), 0, (ty, 0))
        for by in range(1, ny):
            xrecv(dz, (by, 0), 1)
            for tx in range(1, nx):
                xsend(dz, (by, 0), 1, (0, tx))

    def lines(dz):
        for bx in range(1, nx):
            xrecv(dz, (0, bx), 1)
            relay(dz, (0, bx))
        for by in range(1, ny):
            xrecv(dz, (by, 0), 0)
            relay(dz, (by, 0))

    def corners(dz):
        for by in range(1, ny):
            for bx in range(1, nx):
                xrecv(dz, (by, bx), 0)
                xrecv(dz, (by, bx), 1)
                relay(dz, (by, bx))

    hidden_n = wv.shape[1]
    tile = 256

    def product(dz, rc):
        other = xbuf.at[zc(dz), crit(*rc), 1 - k]
        recv(other, ss.at[0], sr.at[ssem(dz, rc)])
        if dz == 0:
            weight_copy(rc).wait()
            if rc == (0, 0):
                own_copy.wait()
                aw_copy.wait()
        first = rc == (0, 0)
        cc = crit(*rc)
        wrows = pl.ds(pl.multiple_of(cc * cols, cols), cols)
        zi = zc(dz)

        def one(i, carry):
            at = pl.ds(pl.multiple_of(i * tile, tile), tile)
            v = jnp.dot(
                xbuf[zi, cc].reshape(2 * rows, cols), wv[wrows, at], preferred_element_type=f32
            )
            if first:
                acc[:, at] = v
            else:
                acc[:, at] += v
            return carry

        lax.fori_loop(0, hidden_n // tile, one, 0)
        v = jnp.dot(
            xbuf[zi, cc].reshape(2 * rows, cols), awv[wrows, :], preferred_element_type=f32
        )
        if first:
            pm[zi] = v
        else:
            pm[zi] += v

    def bins_of(dz):
        hid = jax.nn.silu(acc[...] + b_in[...]).astype(bf16)
        v = jnp.dot(hid, wov[...], preferred_element_type=f32)
        lg[dz] = v.reshape(2, rows, wov.shape[1])
        send(lg.at[dz, 1 - k], rsib.at[dz], ps.at[dz], pr.at[dz], (sib, c))

    def pair_sum(dz):
        recv(rsib.at[dz], ps.at[dz], pr.at[dz])
        psum[dz] = lg[dz, k] + rsib[dz]
        if dz > 0:
            send(psum.at[dz], rz.at[dz], qs.at[dz], qr.at[dz], (zc(dz) * 2 + k, c))

    def spread_rows(m, base):
        t = m.shape[0]
        shape = (t, horizon, m.shape[1])
        keep = iota(shape, 2) == iota(shape, 1) + base
        wide = jnp.where(keep, jnp.broadcast_to(m[:, None, :], shape), 0.0)
        return jnp.sum(wide.reshape(t * horizon, m.shape[1]), axis=-1, keepdims=True)

    def policy(dz):
        zi = zc(dz)
        l = pm[zi]
        e = jnp.exp(l - jnp.max(l, axis=-1, keepdims=True))
        p = e / jnp.sum(e, axis=-1, keepdims=True)
        m = metag[pl.ds(pl.multiple_of(zi * 2 * traj, 2 * traj), 2 * traj), :]
        a = spread_rows(m, horizon)
        hot = (iota(l.shape, 1).astype(f32) == a).astype(f32)
        pm[zi] = p - hot

    def along_z(d):
        send(lat, xbuf.at[z, c, k], zs.at[d], zr.at[d], (zc(nz - d) * 2 + k, c))

    along_z(1)
    enter(0)

    row = iota((traj, 128), 0)
    lane = iota((traj, 128), 1)
    m = jnp.zeros((traj, 128), f32)
    for i in range(traj):
        m = jnp.where((row == i) & (lane == 2 * horizon), ends[i].astype(f32), m)
        m = jnp.where((row == i) & (lane == 2 * horizon + 1), dest[i].astype(f32), m)
    meta[...] = m
    meta[:, 0:horizon] = rewards[...]
    meta[:, horizon : 2 * horizon] = actions[...].astype(f32)
    for d in range(1, nb):
        send(meta, metabuf.at[b], ms.at[d], mr.at[d], batch_peer(d))
    metabuf[b] = meta[...]
    wov[...] = jnp.zeros_like(wov)
    wov[:, 0:bins_n] = w_out[...]

    middle(0)
    if nz > 2:
        along_z(2)
    if nz > 1:
        enter(1)
    lines(0)
    product(0, (0, 0))

    for d in range(1, nb):
        recv(metabuf.at[(b + nb - d) % nb], ms.at[d], mr.at[d])
    everyone = metabuf[...].reshape(total, 128)
    dest_all = everyone[:, 2 * horizon + 1 : 2 * horizon + 2]
    pick = (iota((total, total), 1).astype(f32) == dest_all).astype(f32)
    metag[...] = jnp.dot(pick, everyone, preferred_element_type=f32, precision=HIGHEST)
    mine = (iota((traj, total), 1) == iota((traj, total), 0) + b * traj).astype(f32)
    pick_mine = lax.dot_general(
        mine, pick, (((1,), (1,)), ((), ())), preferred_element_type=f32
    )

    line_blocks = [r for r in rel[1:] if r[0] == 0 or r[1] == 0]
    corner_blocks = [r for r in rel[1:] if r[0] != 0 and r[1] != 0]
    for dz in range(nz):
        if dz > 0:
            product(dz, (0, 0))
        for rc in line_blocks:
            product(dz, rc)
        corners(dz)
        if dz + 1 < nz:
            middle(dz + 1)
            if dz + 3 < nz:
                along_z(dz + 3)
        for rc in corner_blocks:
            product(dz, rc)
        bins_of(dz)
        if dz + 1 < nz:
            lines(dz + 1)
            if dz + 2 < nz:
                enter(dz + 2)
            policy(dz)
            pair_sum(dz)
    pair_sum(nz - 1)
    policy(nz - 1)

    width = grad_out.shape[0]
    start = (b * n + c) * width
    aligned = (start // 128) * 128
    gc = aligned // cols
    goff = pl.multiple_of(aligned % cols, 128)
    xt = xbuf[:, gc, :, :, pl.ds(goff, 128)].reshape(nb * rows, 128).T

    logits = psum[0]
    for d in range(1, nz):
        recv(rz.at[d], qs.at[d], qr.at[d])
        logits = logits + rz[d]
    col = iota(logits.shape, 1)
    real = col < bins_n
    logits = jnp.where(real, logits, -jnp.inf)
    e = jnp.exp(logits - jnp.max(logits, axis=-1, keepdims=True))
    bins = -20.0 + 40.0 * col.astype(f32) / (bins_n - 1)
    value = jnp.sum(e * bins, axis=-1, keepdims=True) / jnp.sum(e, axis=-1, keepdims=True)
    shape = (traj, horizon, 128)
    wide = jnp.broadcast_to(value, (rows, 128)).reshape(shape)
    wide = jnp.where(iota(shape, 2) == iota(shape, 1), wide, 0.0)
    v = jnp.sum(wide, axis=1)
    vown[...] = v
    for i, rc in enumerate(rel[1:]):
        back = ((-rc[0]) % ny) * nx + (-rc[1]) % nx
        send(vown, vbuf.at[back], vs.at[i + 1], vr.at[back], (b, crit(*rc)))
    pay[0] = v
    heats = [-v / smoothing_heat_factor]
    for i in range(1, n):
        recv(vbuf.at[i], vs.at[i], vr.at[i])
        heats.append(-vbuf[i] / smoothing_heat_factor)
    top = functools.reduce(jnp.maximum, heats)
    mean = functools.reduce(jnp.add, [jnp.exp(h - top) for h in heats]) / n
    pay[1] = -smoothing_heat_factor * (top + jnp.log(mean))
    for d in range(1, nb):
        send(pay, sbuf.at[b], bs.at[d], br.at[d], batch_peer(d))
    sbuf[b] = pay[...]
    for d in range(1, nb):
        recv(sbuf.at[(b + nb - d) % nb], bs.at[d], br.at[d])
    values = sbuf[:, 0].reshape(total, 128)
    soft = sbuf[:, 1].reshape(total, 128)

    lane = iota((total, 128), 1)
    step = lane.astype(f32)
    mg = metag[...]
    end = mg[:, 2 * horizon : 2 * horizon + 1]
    live = ((step < end) & (lane < horizon)).astype(f32)
    carry = (step + 1.0 < end).astype(f32)

    def ahead(a, s):
        return pltpu.roll(a, 128 - s, 1)

    decay = future_decay_factor * carry
    inner = lane < horizon - 1
    offset = jnp.where(
        inner,
        mg + decay * (1.0 - blend) * ahead(soft, 1),
        jnp.where(lane == horizon - 1, soft, 0.0),
    )
    factor = jnp.where(inner, decay * blend, 0.0)
    s = 1
    while s < horizon:
        offset = offset + factor * ahead(offset, s)
        factor = factor * ahead(factor, s)
        s *= 2
    raw = jnp.where(lane < horizon, (offset - soft) * live, 0.0)
    square = jnp.sum(jnp.sum(raw * raw, axis=1, keepdims=True), axis=0, keepdims=True)
    lives = jnp.sum(jnp.sum(live, axis=1, keepdims=True), axis=0, keepdims=True)
    scale = jnp.sqrt(square / lives + 1e-06)
    adv = raw / scale

    pull = pm[...].reshape(nb * rows, pm.shape[2]) * spread_rows(adv, 0) / horizon
    grad = jnp.dot(xt, pull.astype(bf16), preferred_element_type=f32)
    if width == 128:
        grad_out[...] = grad
    else:
        gtmp[...] = grad
        grad_out[...] = gtmp[pl.ds(pl.multiple_of(start % 128, width), width), :]
    cv_out[0] = jnp.dot(pick_mine, values, preferred_element_type=f32, precision=HIGHEST)[:, 0:horizon]
    adv_out[...] = jnp.dot(pick_mine, adv, preferred_element_type=f32, precision=HIGHEST)[:, 0:horizon]
    for d in sends:
        d.wait_send()


def on_device(latents, dest, ends, rewards, actions, w_in, b_in, w_out, actor_w):
    nb = lax.axis_size("batch")
    n = lax.axis_size("critic")
    traj, horizon, cols = latents.shape
    rows = traj * horizon
    width, hidden_n = w_in.shape[1:]
    bins_n = w_out.shape[2]
    acts = actor_w.shape[1]
    nx = 1
    while nx * nx * 4 <= n:
        nx *= 2
    ny = n // nx
    if nx * nx < n and nx == 1:
        nx, ny = n, 1
    nz = nb // 2
    lanes = -(-bins_n // 128) * 128
    half_sends = nz * (2 * (nx - 1 + ny - 1) + 2 * (nx - 1) * (ny - 1))
    vmem = pltpu.VMEM
    dma = pltpu.SemaphoreType.DMA
    scratch = [
        vmem((nz, n, 2, rows, cols), bf16),
        vmem((width, hidden_n), bf16),
        vmem((width, acts), bf16),
        vmem((hidden_n, lanes), bf16),
        vmem((2 * rows, hidden_n), f32),
        vmem((nz, 2 * rows, acts), f32),
        vmem((nz, 2, rows, lanes), f32),
        vmem((nz, rows, lanes), f32),
        vmem((nz, rows, lanes), f32),
        vmem((nz, rows, lanes), f32),
        vmem((traj, 128), f32),
        vmem((nb, traj, 128), f32),
        vmem((nb * traj, 128), f32),
        vmem((traj, 128), f32),
        vmem((n, traj, 128), f32),
        vmem((2, traj, 128), f32),
        vmem((nb, 2, traj, 128), f32),
        vmem((128, acts), f32),
        dma((n,)), dma((2,)),
        dma((nz,)), dma((nz,)),
        dma((half_sends,)), dma((nz * n * 2,)),
        dma((nz * n,)), dma((nz * n,)),
        dma((nz,)), dma((nz,)),
        dma((nz,)), dma((nz,)),
        dma((nb,)), dma((nb,)),
        dma((n,)), dma((n,)),
        dma((nb,)), dma((nb,)),
    ]
    inside = pl.BlockSpec(memory_space=pltpu.VMEM)
    scalar = pl.BlockSpec(memory_space=pltpu.SMEM)
    outside = pl.BlockSpec(memory_space=pl.ANY)
    return pl.pallas_call(
        functools.partial(kernel, (nb, n, ny, nx, horizon, bins_n)),
        out_shape=(
            jax.ShapeDtypeStruct((1, traj, horizon), f32),
            jax.ShapeDtypeStruct((traj, horizon), f32),
            jax.ShapeDtypeStruct((width // (nb * n), acts), f32),
        ),
        in_specs=[outside, scalar, scalar, inside, inside, outside, inside, inside, outside],
        out_specs=(inside, inside, inside),
        scratch_shapes=scratch,
        compiler_params=pltpu.CompilerParams(
            collective_id=0, has_side_effects=True, vmem_limit_bytes=60 * 1024 * 1024
        ),
    )(
        latents.reshape(rows, cols), dest, ends, rewards, actions,
        w_in[0], b_in, w_out[0], actor_w,
    )


def solution(mesh):
    placed = (
        P("batch", None, "critic"),
        P("batch"),
        P("batch"),
        P("batch", None),
        P("batch", None),
        P("critic", None, "batch"),
        P("critic", "batch"),
        P("critic", "batch", None),
        P(),
    )
    return jax.shard_map(
        on_device,
        mesh=mesh,
        in_specs=placed,
        out_specs=(P("critic", "batch", None), P("batch", None), P(("batch", "critic"), None)),
        check_vma=False,
    )
```

profile of v0, /device:TPU:0, one launch (start us, length us, event | category | flops | bytes accessed | tf_op | source)
XLA Modules:
  0.0 78.7 jit_solution(16473370832677785060)
XLA Ops:
  0.6 73.9 %shard_map.112 = (f32[1,8,16]{2,1,0:T(8,128)}, f32[8,16]{1,0:T(8,128)}, f32[128,256]{1,0:T(8,128)}) custom-call(bf16[128,1024]{1,0:T(8,128)(2,1)} %bitcast.5, s32[8]{0:T(128)} %dest.1, s32[8]{0:T(128)} %ends.1, f32[8,16]{1,0:T(8,128)} %rewards.1, s32[8,16]{1,0:T(8,128)} %actions.1, bf16[4096,1024]{1,0:T(8,128)(2,1)} %bitcast.3, f32[1,1024]{1,0:T(1,128)} %b_in.1, ...), custom_call_target="tpu_custom_call" | custom-call | tf_op jit(solution)/shard_map/pallas_call | solution.py:415
  74.6 1.3 %copy.15 = f32[1,8,16]{2,1,0:T(8,128)} copy(f32[1,8,16]{2,1,0:T(8,128)} %get-tuple-element.6) | data formatting | bytes 1024
  75.9 1.3 %copy.16 = f32[8,16]{1,0:T(8,128)} copy(f32[8,16]{1,0:T(8,128)} %get-tuple-element.7) | data formatting | bytes 1024
  77.1 1.6 %copy.17 = f32[128,256]{1,0:T(8,128)} copy(f32[128,256]{1,0:T(8,128)} %get-tuple-element.8) | data formatting | bytes 262144
where the time goes:
time: 78.9 us; the launch traced here: 78.7 us
  Pallas kernels  73.9 us (94%)
  local copies, waits for them, and re-layouts  4.11 us (5%)
    pallas_call x1, Pallas kernels, on_device(): pl.pallas_call(functools.partial(kernel, (nb, n, ny, nx, horizon, bins_n)...  73.9 us
    unnamed x3, local copies, waits for them, and re-layouts  4.11 us

commit v1 on v0

--- a/solution.py
+++ b/solution.py
@@ -359,6 +359,440 @@
     adv_out[...] = jnp.dot(pick_mine, adv, preferred_element_type=f32, precision=HIGHEST)[:, 0:horizon]
     for d in sends:
         d.wait_send()
+
+
+def plane_kernel(
+    sizes, lat, dest, ends, rewards, actions, w_hbm, b_in, w_out, aw_hbm,
+    cv_out, adv_out, grad_out,
+    xbuf, wv, wov, acc, pm, lg, psum, rsib, rz, meta, metabuf, metag,
+    vown, vbuf, pay, sbuf,
+    wsem, lsem, zs, zr, xs, xr, ss, sr, ps, pr, qs, qr, ms, mr, vs, vr, bs, br,
+):
+    nb, n, horizon, bins_n = sizes
+    nz = nb // 2
+    rows, cols = lat.shape
+    half = rows // 2
+    traj = rows // horizon
+    total = nb * traj
+    hidden_n = w_hbm.shape[1]
+    acts = aw_hbm.shape[1]
+    b = lax.axis_index("batch")
+    c = lax.axis_index("critic")
+    z, k = b // 2, b % 2
+    y, x = c // 2, c % 2
+    sib = z * 2 + (1 - k)
+    col = [c, y * 2 + (1 - x), (1 - y) * 2 + x, (1 - y) * 2 + (1 - x)]
+    sends = []
+
+    def closeness(i):
+        side = 1 if i < nz / 2 else -1
+        return sorted(range(nz), key=lambda p: (abs(p - i), side * (i - p)))
+
+    def pick(values):
+        v = jnp.int32(values[0])
+        for i in range(1, nz):
+            v = jnp.where(z == i, jnp.int32(values[i]), v)
+        return v
+
+    orders = [closeness(i) for i in range(nz)]
+    plane = [z] + [pick([orders[i][s] for i in range(nz)]) for s in range(1, nz)]
+
+    def batch_peer(d):
+        return ((b + d) % nb, c)
+
+    def wcopy(q):
+        at = pl.ds(pl.multiple_of(col[q] * cols, cols), cols)
+        return (
+            pltpu.make_async_copy(
+                w_hbm.at[at], wv.at[at, pl.ds(0, hidden_n)], wsem.at[q]
+            ),
+            pltpu.make_async_copy(
+                aw_hbm.at[at], wv.at[at, pl.ds(hidden_n, acts)], wsem.at[4 + q]
+            ),
+        )
+
+    for d in wcopy(0):
+        d.start()
+    own_copy = pltpu.make_async_copy(lat, xbuf.at[z, c, k], lsem.at[0])
+    own_copy.start()
+
+    below, above = z > 0, z < nz - 1
+    barrier = pltpu.get_barrier_semaphore()
+
+    def greet(dev):
+        pl.semaphore_signal(barrier, inc=1, device_id=dev, device_id_type=MESH)
+
+    greet((sib, c))
+    greet((b, col[1]))
+    greet((b, col[2]))
+
+    @pl.when(below)
+    def _():
+        greet(((z - 1) * 2 + k, c))
+
+    @pl.when(above)
+    def _():
+        greet(((z + 1) * 2 + k, c))
+
+    pl.semaphore_wait(barrier, 3 + jnp.where(below, 1, 0) + jnp.where(above, 1, 0))
+
+    def send(src, dst, s, r, dev, when=None):
+        d = pltpu.make_async_remote_copy(
+            src_ref=src, dst_ref=dst, send_sem=s, recv_sem=r, device_id=dev, device_id_type=MESH
+        )
+        if when is None:
+            d.start()
+        else:
+            pl.when(when)(d.start)
+        sends.append((d, when))
+
+    def recv(dst, s, r):
+        pltpu.make_async_remote_copy(
+            src_ref=dst, dst_ref=dst, send_sem=s, recv_sem=r,
+            device_id=(sib, c), device_id_type=MESH,
+        ).wait_recv()
+
+    def hrow(h):
+        return pl.ds(h * half, half)
+
+    def block(s, q, h=None):
+        if h is None:
+            return xbuf.at[plane[s], col[q], k]
+        return xbuf.at[plane[s], col[q], k, hrow(h)]
+
+    def across(s, h):
+        src = lat.at[hrow(h)] if s == 0 else block(s, 0, h)
+        for j in (1, 2):
+            i = (s * 3 + (j - 1)) * 2 + h
+            send(src, block(s, 0, h), xs.at[i], xr.at[i], (b, col[j]))
+
+    def onward(s):
+        for j in (1, 2):
+            i = (s * 3 + 2) * 2 + (j - 1)
+            at = block(s, 3 - j, j - 1)
+            send(at, at, xs.at[i], xr.at[i], (b, col[j]))
+
+    def arrived(s, q):
+        for h in range(2):
+            i = (s * 3 + (q - 1)) * 2 + h
+            recv(block(s, q, h), xs.at[0], xr.at[i])
+
+    def relay(s, q):
+        src = lat if s == 0 and q == 0 else block(s, q)
+        send(src, block(s, q), ss.at[s * 4 + q], sr.at[s * 4 + q], (sib, c))
+
+    def along(h):
+        for j, (dz, ok) in enumerate(((-1, below), (1, above))):
+            send(
+                lat.at[hrow(h)], xbuf.at[z, c, k, hrow(h)],
+                zs.at[j * 2 + h], zr.at[z * 2 + h], ((z + dz) * 2 + k, c), ok,
+            )
+
+    def passed(d, h):
+        for j, sg in enumerate((-1, 1)):
+            p = z + sg * d
+            there = (p >= 0) & (p < nz)
+            on = z - sg
+            at = xbuf.at[p, c, k, hrow(h)]
+
+            @pl.when(there)
+            def _():
+                recv(at, zs.at[0], zr.at[p * 2 + h])
+
+            if d < nz - 1:
+                send(
+                    at, at, zs.at[(d * 2 + j) * 2 + h], zr.at[p * 2 + h],
+                    (on * 2 + k, c), there & (on >= 0) & (on < nz),
+                )
+
+    tile = 256
+    tiles = (hidden_n + acts) // tile
+
+    def product(s, q, first=False):
+        p, cc = plane[s], col[q]
+        recv(xbuf.at[p, cc, 1 - k], ss.at[0], sr.at[s * 4 + q])
+        wrows = pl.ds(pl.multiple_of(cc * cols, cols), cols)
+
+        def one(i, carry):
+            at = pl.ds(pl.multiple_of(i * tile, tile), tile)
+            v = jnp.dot(
+                xbuf[p, cc].reshape(2 * rows, cols), wv[wrows, at], preferred_element_type=f32
+            )
+            if first:
+                acc[s, :, at] = v
+            else:
+                acc[s, :, at] += v
+            return carry
+
+        lax.fori_loop(0, tiles, one, 0)
+
+    def bins_of(s):
+        hid = jax.nn.silu(acc[s, :, 0:hidden_n] + b_in[...]).astype(bf16)
+        v = jnp.dot(hid, wov[...], preferred_element_type=f32)
+        lg[s] = v.reshape(2, rows, wov.shape[1])
+        send(lg.at[s, 1 - k], rsib.at[s], ps.at[s], pr.at[s], (sib, c))
+
+    def pair_sum(s):
+        recv(rsib.at[s], ps.at[s], pr.at[s])
+        psum[s] = lg[s, k] + rsib[s]
+        if s > 0:
+            send(psum.at[s], rz.at[z], qs.at[s], qr.at[z], (plane[s] * 2 + k, c))
+
+    def spread_rows(m, base):
+        t = m.shape[0]
+        shape = (t, horizon, m.shape[1])
+        keep = iota(shape, 2) == iota(shape, 1) + base
+        wide = jnp.where(keep, jnp.broadcast_to(m[:, None, :], shape), 0.0)
+        return jnp.sum(wide.reshape(t * horizon, m.shape[1]), axis=-1, keepdims=True)
+
+    def policy(s):
+        p = plane[s]
+        l = acc[s, :, hidden_n : hidden_n + acts]
+        e = jnp.exp(l - jnp.max(l, axis=-1, keepdims=True))
+        prob = e / jnp.sum(e, axis=-1, keepdims=True)
+        m = metag[pl.ds(pl.multiple_of(p * 2 * traj, 2 * traj), 2 * traj), :]
+        a = spread_rows(m, horizon)
+        hot = (iota(l.shape, 1).astype(f32) == a).astype(f32)
+        pm[p] = prob - hot
+
+    along(0)
+    across(0, 0)
+    relay(0, 0)
+    along(1)
+    across(0, 1)
+    for q in range(1, 4):
+        for d in wcopy(q):
+            d.start()
+
+    row = iota((traj, 128), 0)
+    lane = iota((traj, 128), 1)
+    m = jnp.zeros((traj, 128), f32)
+    for i in range(traj):
+        m = jnp.where((row == i) & (lane == 2 * horizon), ends[i].astype(f32), m)
+        m = jnp.where((row == i) & (lane == 2 * horizon + 1), dest[i].astype(f32), m)
+    meta[...] = m
+    meta[:, 0:horizon] = rewards[...]
+    meta[:, horizon : 2 * horizon] = actions[...].astype(f32)
+    metabuf[b] = meta[...]
+    wov[...] = jnp.zeros_like(wov)
+    wov[:, 0:bins_n] = w_out[...]
+
+    def ready(q):
+        for d in wcopy(q):
+            d.wait()
+
+    own_copy.wait()
+    ready(0)
+    product(0, 0, True)
+    for q in range(1, 4):
+        ready(q)
+    passed(1, 0)
+    across(1, 0)
+    passed(1, 1)
+    across(1, 1)
+    relay(1, 0)
+    for q in (1, 2):
+        arrived(0, q)
+        relay(0, q)
+    for s in range(2, nz):
+        product(s - 1, 0, True)
+        product(s - 2, 1)
+        passed(s, 0)
+        across(s, 0)
+        product(s - 2, 2)
+        passed(s, 1)
+        across(s, 1)
+        relay(s, 0)
+        for q in (1, 2):
+            arrived(s - 1, q)
+            relay(s - 1, q)
+    order = [nz - 2] + list(range(1, nz - 2)) + [nz - 1, 0]
+    for s in order[:-2]:
+        onward(s)
+    product(nz - 1, 0, True)
+    for d in range(1, nb):
+        send(meta, metabuf.at[b], ms.at[d], mr.at[d], batch_peer(d))
+    for q in (1, 2):
+        product(nz - 2, q)
+    for q in (1, 2):
+        arrived(nz - 1, q)
+        relay(nz - 1, q)
+    onward(nz - 1)
+    onward(0)
+
+    for d in range(1, nb):
+        recv(metabuf.at[(b + nb - d) % nb], ms.at[d], mr.at[d])
+    everyone = metabuf[...].reshape(total, 128)
+    dest_all = everyone[:, 2 * horizon + 1 : 2 * horizon + 2]
+    pickm = (iota((total, total), 1).astype(f32) == dest_all).astype(f32)
+    metag[...] = jnp.dot(pickm, everyone, preferred_element_type=f32, precision=HIGHEST)
+    mine = (iota((traj, total), 1) == iota((traj, total), 0) + b * traj).astype(f32)
+    pick_mine = lax.dot_general(
+        mine, pickm, (((1,), (1,)), ((), ())), preferred_element_type=f32
+    )
+    for q in (1, 2):
+        product(nz - 1, q)
+
+    before = None
+    for s in order:
+        arrived(s, 3)
+        relay(s, 3)
+        if before is not None:
+            pair_sum(before)
+        product(s, 3)
+        bins_of(s)
+        if s != order[-1]:
+            policy(s)
+        before = s
+    policy(before)
+    gc = ((b * n + c) * grad_out.shape[0]) // cols
+    goff = pl.multiple_of(((b * n + c) * grad_out.shape[0]) % cols, 128)
+    xt = xbuf[:, gc, :, :, pl.ds(goff, 128)].reshape(nb * rows, 128).T
+    pair_sum(before)
+
+    logits = psum[0]
+    for d in range(1, nz):
+        o = (z + d) % nz
+        recv(rz.at[o], qs.at[0], qr.at[o])
+        logits = logits + rz[o]
+    lane2 = iota(logits.shape, 1)
+    real = lane2 < bins_n
+    logits = jnp.where(real, logits, -jnp.inf)
+    e = jnp.exp(logits - jnp.max(logits, axis=-1, keepdims=True))
+    bins = -20.0 + 40.0 * lane2.astype(f32) / (bins_n - 1)
+    value = jnp.sum(e * bins, axis=-1, keepdims=True) / jnp.sum(e, axis=-1, keepdims=True)
+    shape = (traj, horizon, 128)
+    wide = jnp.broadcast_to(value, (rows, 128)).reshape(shape)
+    wide = jnp.where(iota(shape, 2) == iota(shape, 1), wide, 0.0)
+    v = jnp.sum(wide, axis=1)
+    vown[...] = v
+    for i in range(1, n):
+        send(vown, vbuf.at[i], vs.at[i], vr.at[i], (b, col[i]))
+    pay[0] = v
+    heats = [-v / smoothing_heat_factor]
+    for i in range(1, n):
+        recv(vbuf.at[i], vs.at[i], vr.at[i])
+        heats.append(-vbuf[i] / smoothing_heat_factor)
+    top = functools.reduce(jnp.maximum, heats)
+    mean = functools.reduce(jnp.add, [jnp.exp(h - top) for h in heats]) / n
+    pay[1] = -smoothing_heat_factor * (top + jnp.log(mean))
+    for d in range(1, nb):
+        send(pay, sbuf.at[b], bs.at[d], br.at[d], batch_peer(d))
+    sbuf[b] = pay[...]
+    for d in range(1, nb):
+        recv(sbuf.at[(b + nb - d) % nb], bs.at[d], br.at[d])
+    values = sbuf[:, 0].reshape(total, 128)
+    soft = sbuf[:, 1].reshape(total, 128)
+
+    lane = iota((total, 128), 1)
+    step = lane.astype(f32)
+    mg = metag[...]
+    end = mg[:, 2 * horizon : 2 * horizon + 1]
+    live = ((step < end) & (lane < horizon)).astype(f32)
+    carry = (step + 1.0 < end).astype(f32)
+
+    def ahead(a, s):
+        return pltpu.roll(a, 128 - s, 1)
+
+    decay = future_decay_factor * carry
+    inner = lane < horizon - 1
+    offset = jnp.where(
+        inner,
+        mg + decay * (1.0 - blend) * ahead(soft, 1),
+        jnp.where(lane == horizon - 1, soft, 0.0),
+    )
+    factor = jnp.where(inner, decay * blend, 0.0)
+    s = 1
+    while s < horizon:
+        offset = offset + factor * ahead(offset, s)
+        factor = factor * ahead(factor, s)
+        s *= 2
+    raw = jnp.where(lane < horizon, (offset - soft) * live, 0.0)
+    square = jnp.sum(jnp.sum(raw * raw, axis=1, keepdims=True), axis=0, keepdims=True)
+    lives = jnp.sum(jnp.sum(live, axis=1, keepdims=True), axis=0, keepdims=True)
+    scale = jnp.sqrt(square / lives + 1e-06)
+    adv = raw / scale
+
+    pull = pm[...].reshape(nb * rows, pm.shape[2]) * spread_rows(adv, 0) / horizon
+    grad_out[...] = jnp.dot(xt, pull.astype(bf16), preferred_element_type=f32)
+    cv_out[0] = jnp.dot(pick_mine, values, preferred_element_type=f32, precision=HIGHEST)[:, 0:horizon]
+    adv_out[...] = jnp.dot(pick_mine, adv, preferred_element_type=f32, precision=HIGHEST)[:, 0:horizon]
+    for d, when in sends:
+        if when is None:
+            d.wait_send()
+        else:
+            pl.when(when)(d.wait_send)
+
+
+def hand_over(cv, adv, grad, cv_out, adv_out, grad_out):
+    cv_out[...] = cv[...]
+    adv_out[...] = adv[...]
+    grad_out[...] = grad[...]
+
+
+def on_planes(latents, dest, ends, rewards, actions, w_in, b_in, w_out, actor_w):
+    nb = lax.axis_size("batch")
+    n = lax.axis_size("critic")
+    traj, horizon, cols = latents.shape
+    rows = traj * horizon
+    width, hidden_n = w_in.shape[1:]
+    bins_n = w_out.shape[2]
+    acts = actor_w.shape[1]
+    nz = nb // 2
+    lanes = -(-bins_n // 128) * 128
+    vmem = pltpu.VMEM
+    dma = pltpu.SemaphoreType.DMA
+    scratch = [
+        vmem((nz, n, 2, rows, cols), bf16),
+        vmem((width, hidden_n + acts), bf16),
+        vmem((hidden_n, lanes), bf16),
+        vmem((nz, 2 * rows, hidden_n + acts), f32),
+        vmem((nz, 2 * rows, acts), f32),
+        vmem((nz, 2, rows, lanes), f32),
+        vmem((nz, rows, lanes), f32),
+        vmem((nz, rows, lanes), f32),
+        vmem((nz, rows, lanes), f32),
+        vmem((traj, 128), f32),
+        vmem((nb, traj, 128), f32),
+        vmem((nb * traj, 128), f32),
+        vmem((traj, 128), f32),
+        vmem((n, traj, 128), f32),
+        vmem((2, traj, 128), f32),
+        vmem((nb, 2, traj, 128), f32),
+        dma((2 * n,)), dma((1,)),
+        dma((nz * 4,)), dma((nz * 2,)),
+        dma((nz * 6,)), dma((nz * 6,)),
+        dma((nz * n,)), dma((nz * n,)),
+        dma((nz,)), dma((nz,)),
+        dma((nz,)), dma((nz,)),
+        dma((nb,)), dma((nb,)),
+        dma((n,)), dma((n,)),
+        dma((nb,)), dma((nb,)),
+    ]
+    inside = pl.BlockSpec(memory_space=pltpu.VMEM)
+    scalar = pl.BlockSpec(memory_space=pltpu.SMEM)
+    outside = pl.BlockSpec(memory_space=pl.ANY)
+    shapes = (
+        jax.ShapeDtypeStruct((1, traj, horizon), f32),
+        jax.ShapeDtypeStruct((traj, horizon), f32),
+        jax.ShapeDtypeStruct((width // (nb * n), acts), f32),
+    )
+    out = pl.pallas_call(
+        functools.partial(plane_kernel, (nb, n, horizon, bins_n)),
+        out_shape=shapes,
+        in_specs=[outside, scalar, scalar, inside, inside, outside, inside, inside, outside],
+        out_specs=(inside, inside, inside),
+        scratch_shapes=scratch,
+        compiler_params=pltpu.CompilerParams(
+            collective_id=0, has_side_effects=True, vmem_limit_bytes=60 * 1024 * 1024
+        ),
+    )(
+        latents.reshape(rows, cols), dest, ends, rewards, actions,
+        w_in[0], b_in, w_out[0], actor_w,
+    )
+    return pl.pallas_call(
+        hand_over, out_shape=shapes, in_specs=[inside] * 3, out_specs=(inside,) * 3
+    )(*out)
 
 
 def on_device(latents, dest, ends, rewards, actions, w_in, b_in, w_out, actor_w):
@@ -443,8 +877,9 @@
         P("critic", "batch", None),
         P(),
     )
+    planes = mesh.shape["batch"] == 8 and mesh.shape["critic"] == 4
     return jax.shard_map(
-        on_device,
+        on_planes if planes else on_device,
         mesh=mesh,
         in_specs=placed,
         out_specs=(P("critic", "batch", None), P("batch", None), P(("batch", "critic"), None)),

time: 78.9 us -> 68.7 us (0.87)
  Pallas kernels: 73.9 us -> 67.9 us
  local copies, waits for them, and re-layouts: 4.11 us -> 0 us
    pallas_call x1 -> x2, Pallas kernels: 73.9 us -> 67.9 us  [the longest x1 66.3 us: on_planes(): pl.pallas_call(functools.partial(plane_kernel, (nb, n, horizon, bins_n)),...]
    unnamed x3 -> x0, local copies, waits for them, and re-layouts: 4.11 us -> none
where the time goes in v1:
time: 68.7 us; the launch traced here: 68.6 us
  Pallas kernels  67.9 us (99%)
    pallas_call x1, Pallas kernels, on_planes(): pl.pallas_call(functools.partial(plane_kernel, (nb, n, horizon, bins_n)),...  66.3 us
    pallas_call x1, Pallas kernels, on_planes(): pl.pallas_call(hand_over, out_shape=shapes, in_specs=[inside] * 3, out_sp...  1.58 us

profile of v1, /device:TPU:0, one launch (start us, length us, event | category | flops | bytes accessed | tf_op | source)
XLA Modules:
  0.0 68.6 jit_solution(17810420846911532877)
XLA Ops:
  0.6 66.3 %shard_map.112 = (f32[1,8,16]{2,1,0:T(8,128)}, f32[8,16]{1,0:T(8,128)}, f32[128,256]{1,0:T(8,128)}) custom-call(bf16[128,1024]{1,0:T(8,128)(2,1)} %bitcast.5, s32[8]{0:T(128)} %dest.1, s32[8]{0:T(128)} %ends.1, f32[8,16]{1,0:T(8,128)} %rewards.1, s32[8,16]{1,0:T(8,128)} %actions.1, bf16[4096,1024]{1,0:T(8,128)(2,1)} %bitcast.3, f32[1,1024]{1,0:T(1,128)} %b_in.1, ...), custom_call_target="tpu_custom_call" | custom-call | tf_op jit(solution)/shard_map/pallas_call | solution.py:780
  67.0 1.6 %shard_map.113 = (f32[1,8,16]{2,1,0:T(8,128)}, f32[8,16]{1,0:T(8,128)}, f32[128,256]{1,0:T(8,128)}) custom-call(f32[1,8,16]{2,1,0:T(8,128)} %get-tuple-element.6.cv, f32[8,16]{1,0:T(8,128)} %get-tuple-element.7.adv, f32[128,256]{1,0:T(8,128)} %get-tuple-element.8.grad), custom_call_target="tpu_custom_call" | custom-call | tf_op jit(solution)/shard_map/pallas_call | solution.py:793

commit v2 on v1

--- a/solution.py
+++ b/solution.py
@@ -505,26 +505,18 @@
                     (on * 2 + k, c), there & (on >= 0) & (on < nz),
                 )
 
-    tile = 256
-    tiles = (hidden_n + acts) // tile
-
     def product(s, q, first=False):
         p, cc = plane[s], col[q]
         recv(xbuf.at[p, cc, 1 - k], ss.at[0], sr.at[s * 4 + q])
         wrows = pl.ds(pl.multiple_of(cc * cols, cols), cols)
 
-        def one(i, carry):
-            at = pl.ds(pl.multiple_of(i * tile, tile), tile)
-            v = jnp.dot(
-                xbuf[p, cc].reshape(2 * rows, cols), wv[wrows, at], preferred_element_type=f32
-            )
-            if first:
-                acc[s, :, at] = v
-            else:
-                acc[s, :, at] += v
-            return carry
-
-        lax.fori_loop(0, tiles, one, 0)
+        v = jnp.dot(
+            xbuf[p, cc].reshape(2 * rows, cols), wv[wrows, :], preferred_element_type=f32
+        )
+        if first:
+            acc[s] = v
+        else:
+            acc[s] += v
 
     def bins_of(s):
         hid = jax.nn.silu(acc[s, :, 0:hidden_n] + b_in[...]).astype(bf16)

time: 68.7 us -> 64.1 us (0.933)
  Pallas kernels: 67.9 us -> 63.3 us
    pallas_call x1, Pallas kernels: 66.3 us -> 61.7 us  [on_planes(): pl.pallas_call(functools.partial(plane_kernel, (nb, n, horizon, bins_n)),...]
where the time goes in v2:
time: 64.1 us; the launch traced here: 63.9 us
  Pallas kernels  63.3 us (99%)
    pallas_call x1, Pallas kernels, on_planes(): pl.pallas_call(functools.partial(plane_kernel, (nb, n, horizon, bins_n)),...  61.7 us
    pallas_call x1, Pallas kernels, on_planes(): pl.pallas_call(hand_over, out_shape=shapes, in_specs=[inside] * 3, out_sp...  1.58 us

profile of v2, /device:TPU:0, one launch (start us, length us, event | category | flops | bytes accessed | tf_op | source)
XLA Modules:
  0.0 63.9 jit_solution(6244862251837302703)
XLA Ops:
  0.6 61.7 %shard_map.112 = (f32[1,8,16]{2,1,0:T(8,128)}, f32[8,16]{1,0:T(8,128)}, f32[128,256]{1,0:T(8,128)}) custom-call(bf16[128,1024]{1,0:T(8,128)(2,1)} %bitcast.5, s32[8]{0:T(128)} %dest.1, s32[8]{0:T(128)} %ends.1, f32[8,16]{1,0:T(8,128)} %rewards.1, s32[8,16]{1,0:T(8,128)} %actions.1, bf16[4096,1024]{1,0:T(8,128)(2,1)} %bitcast.3, f32[1,1024]{1,0:T(1,128)} %b_in.1, ...), custom_call_target="tpu_custom_call" | custom-call | tf_op jit(solution)/shard_map/pallas_call | solution.py:772
  62.4 1.6 %shard_map.113 = (f32[1,8,16]{2,1,0:T(8,128)}, f32[8,16]{1,0:T(8,128)}, f32[128,256]{1,0:T(8,128)}) custom-call(f32[1,8,16]{2,1,0:T(8,128)} %get-tuple-element.6.cv, f32[8,16]{1,0:T(8,128)} %get-tuple-element.7.adv, f32[128,256]{1,0:T(8,128)} %get-tuple-element.8.grad), custom_call_target="tpu_custom_call" | custom-call | tf_op jit(solution)/shard_map/pallas_call | solution.py:785
